TPU v7x, 256 devices: a whole 4x4x8 slice. The times are simulated.
256 devices in a mesh: dp: 32 (over x, z), mp: 8 (over y, core).
Axes of the slice: x: 4, y: 4, z: 8, core: 2. Of those that a mesh axis runs over, the one named last changes fastest.
Arguments:
- grad_parts: bfloat16 [32, 16, 1024, 1024], P('dp', None, None, 'mp'), may hold values from -6 to 6
- owners: int32 [16], replicated, may hold values from 0 to 7, as said below
- left_stat: float32 [32, 1024, 1024], P('mp', 'dp'), may hold values from -1 to 8
- right_stat: float32 [32, 1024, 1024], P('mp', 'dp'), may hold values from -1 to 8
- left_root: bfloat16 [32, 1024, 1024], P('mp', 'dp'), may hold values from -1 to 9
- right_root: bfloat16 [32, 1024, 1024], P('mp'), may hold values from -1 to 3
- first_moment: float32 [32, 1024, 1024], P('mp', 'dp'), may hold values from -32 to 32
- second_moment: float32 [32, 1024, 1024], P('mp', 'dp'), may hold values from 0.5 to 2
- vec_grad: bfloat16 [32, 73728], P('dp', 'mp'), may hold values from -3 to 3
- vec_first: float32 [73728], P('mp'), may hold values from -4 to 4
- vec_second: float32 [73728], P('mp'), may hold values from 0.5 to 2
Outputs:
- block_update: bfloat16 [16, 1024, 1024], P(None, 'dp', 'mp')
- left_new: float32 [32, 1024, 1024], P('mp', 'dp')
- right_new: float32 [32, 1024, 1024], P('mp', 'dp')
- first_new: float32 [32, 1024, 1024], P('mp', 'dp')
- second_new: float32 [32, 1024, 1024], P('mp', 'dp')
- vec_update: bfloat16 [73728], P('mp')
- vec_first_new: float32 [73728], P('mp')
- vec_second_new: float32 [73728], P('mp')
Inputs may be any that keep to these rules, and one draw needn't show every extreme that they name: `owners`: no owner holds more than 4 blocks, and in every draw some owner holds exactly 4.
All inputs are finite; a program needn't handle non-finite values.
Results may differ from a plain program's by a relative error of at most 0.018.
Values may be sent and summed in bfloat16 or wider, within the bound.
A program may use at most 128 MiB of HBM per device.

v0:
```python
import jax
import jax.numpy as jnp
from jax import lax
from jax.sharding import PartitionSpec as P

beta_one = 0.9
beta_two = 0.95
adam_eps = 1e-08
graft_eps = 1e-06


def owner_table(owners, owner_count, slot_count):
    block_count = owners.shape[0]
    same = owners[:, None] == owners[None, :]
    earlier = lax.broadcasted_iota(jnp.int32, (block_count, block_count), 1) < lax.broadcasted_iota(
        jnp.int32, (block_count, block_count), 0
    )
    slots = jnp.sum((same & earlier).astype(jnp.int32), axis=1)
    owner_ids = lax.broadcasted_iota(jnp.int32, (owner_count, slot_count, block_count), 0)
    slot_ids = lax.broadcasted_iota(jnp.int32, (owner_count, slot_count, block_count), 1)
    return ((owners[None, None, :] == owner_ids) & (slots[None, None, :] == slot_ids)).astype(
        jnp.float32
    )


def body(
    grad_parts,
    owners,
    left_stat,
    right_stat,
    left_root,
    right_root,
    first_moment,
    second_moment,
    vec_grad,
    vec_first,
    vec_second,
):
    owner_count = lax.axis_size("mp")
    slot_count, row_count, order = left_stat.shape
    col_count = order // owner_count
    my_rows = lax.axis_index("dp") * row_count
    my_owner = lax.axis_index("mp")
    row_pieces = lax.psum_scatter(
        grad_parts[0].astype(jnp.float32).astype(jnp.bfloat16),
        "dp",
        scatter_dimension=1,
        tiled=True,
    ).astype(jnp.float32)
    selector = owner_table(owners, owner_count, slot_count)
    outgoing = jnp.einsum("ocb,brw->crow", selector, row_pieces, precision=lax.Precision.HIGHEST)
    incoming = lax.all_to_all(
        outgoing.astype(jnp.bfloat16), "mp", split_axis=2, concat_axis=2, tiled=True
    ).astype(outgoing.dtype)
    grad_rows = incoming.reshape(slot_count, row_count, order)
    mine = lax.dynamic_index_in_dim(selector, my_owner, 0, keepdims=False)
    used_mask = (jnp.sum(mine, axis=1) > 0.5)[:, None, None]
    rounded_rows = grad_rows.astype(jnp.bfloat16)
    shard_rows = lax.all_gather(rounded_rows, "dp", axis=1, tiled=True)
    left_part = jnp.einsum(
        "crk,cnk->crn", rounded_rows, shard_rows, preferred_element_type=jnp.float32
    )
    own_cols = lax.dynamic_slice_in_dim(shard_rows, my_rows, row_count, 2)
    right_acc = jnp.einsum("cnr,cnk->crk", own_cols, shard_rows, preferred_element_type=jnp.float32)
    applied_acc = jnp.einsum(
        "crn,cnk->crk", left_root, shard_rows, preferred_element_type=jnp.float32
    )
    scale = 1.0 / order
    left_new = jnp.where(used_mask, left_stat + left_part * scale, left_stat)
    right_new = jnp.where(used_mask, right_stat + right_acc * scale, right_stat)
    first_new = jnp.where(
        used_mask, beta_one * first_moment + (1.0 - beta_one) * grad_rows, first_moment
    )
    second_new = jnp.where(
        used_mask,
        beta_two * second_moment + (1.0 - beta_two) * grad_rows * grad_rows,
        second_moment,
    )
    adam = first_new / (jnp.sqrt(second_new) + adam_eps)
    precond = jnp.einsum(
        "crk,ckm->crm",
        applied_acc.astype(jnp.bfloat16),
        right_root,
        preferred_element_type=jnp.float32,
    )
    square_adam = jnp.sum(adam * adam, axis=(1, 2))
    square_pre = jnp.sum(precond * precond, axis=(1, 2))
    squares = lax.all_gather(jnp.stack([square_adam, square_pre]), "dp")
    square_adam, square_pre = jnp.sum(squares, axis=0)
    vec_all = lax.all_gather(vec_grad[0], "dp")
    vec_sum = jnp.sum(vec_all.astype(jnp.float32), axis=0)
    cells = float(order * order)
    graft = jnp.sqrt(square_adam / cells) / jnp.sqrt(square_pre / cells + graft_eps)
    update_rows = (precond * graft[:, None, None]).astype(jnp.bfloat16)
    returned = lax.all_to_all(
        update_rows.reshape(slot_count, row_count, owner_count, col_count),
        "mp",
        split_axis=2,
        concat_axis=2,
        tiled=True,
    )
    block_update = jnp.einsum(
        "ocb,crow->brw", selector.astype(jnp.bfloat16), returned, preferred_element_type=jnp.float32
    ).astype(jnp.bfloat16)
    vec_first_new = beta_one * vec_first + (1.0 - beta_one) * vec_sum
    vec_second_new = beta_two * vec_second + (1.0 - beta_two) * vec_sum * vec_sum
    vec_update = (vec_first_new / (jnp.sqrt(vec_second_new) + adam_eps)).astype(jnp.bfloat16)
    return (
        block_update,
        left_new,
        right_new,
        first_new,
        second_new,
        vec_update,
        vec_first_new,
        vec_second_new,
    )


def solution(mesh):
    placed = (
        P("dp", None, None, "mp"),
        P(),
        P("mp", "dp", None),
        P("mp", "dp", None),
        P("mp", "dp", None),
        P("mp", None, None),
        P("mp", "dp", None),
        P("mp", "dp", None),
        P("dp", "mp"),
        P("mp"),
        P("mp"),
    )
    return jax.shard_map(
        body,
        mesh=mesh,
        in_specs=placed,
        out_specs=(
            P(None, "dp", "mp"),
            P("mp", "dp", None),
            P("mp", "dp", None),
            P("mp", "dp", None),
            P("mp", "dp", None),
            P("mp"),
            P("mp"),
            P("mp"),
        ),
        check_vma=False,
    )
```

profile of v0, /device:TPU:1, one launch (start us, length us, event | category | flops | bytes accessed | tf_op | source)
XLA Modules:
  0.0 420.2 jit_solution(11740701285527777204)
XLA Ops:
  7.2 0.0 copy-start
  7.2 0.0 copy-start.6
  7.2 0.0 copy-start.7
  7.2 0.0 copy-start.3
  7.2 0.0 copy-start.4
  7.2 0.0 reduce-scatter.2.cloned.1.call-start
  7.3 0.7 reduce-scatter.2.cloned.1.call-update
  8.0 0.0 all-gather.5.cloned.1.call-start
  8.0 0.9 convert_reduce_fusion.1
  8.9 223.8 %reduce-scatter.2.cloned.1.call-done = bf16[16,32,128]{2,1,0:T(8,128)(2,1)} async-done(((bf16[16,1024,128]{2,1,0:T(8,128)(2,1)}), bf16[16,32,128]{2,1,0:T(8,128)(2,1)}) %reduce-scatter.2.cloned.1.call-update) | async-done | bytes 131088 | tf_op jit(solution)/shard_map/reduce_scatter | solution.py:44
  232.8 1.1 fusion.4
  233.9 16.5 %all_to_all.10 = bf16[4,32,8,128]{3,1,0,2:T(8,128)(2,1)S(1)} all-to-all(bf16[4,32,8,128]{3,1,0,2:T(8,128)(2,1)S(1)} %copy.31), channel_id=1, replica_groups=mesh['dp'=32,'mp'=8] {'mp'}, dimensions={2} | all-to-all | bytes 524288 | tf_op jit(solution)/shard_map/all_to_all | solution.py:52
  250.4 0.7 copy_bitcast_fusion
  251.2 0.0 all-gather.5.cloned.1.call-update
  251.2 0.7 fusion.19
  251.9 0.1 dynamic-slice_reduce_fusion
  252.0 39.8 %all-gather.2 = bf16[32,1,9216]{2,1,0:T(2,128)(2,1)S(1)} all-gather(bf16[1,1,9216]{2,1,0:T(2,128)(2,1)} %bitcast.55), channel_id=1, replica_groups=mesh['dp'=32,'mp'=8] {'dp'}, dimensions={0}, use_global_device_ids=true | all-gather | bytes 608256 | tf_op jit(solution)/shard_map/all_gather | solution.py:90
  291.8 1.3 convert_reduce_fusion
  293.1 0.0 copy-done.6
  293.1 0.0 copy-done.7
  293.1 0.6 divide_convert_fusion
  293.8 0.0 copy-done.3
  293.8 0.0 copy-done.4
  293.8 1.4 multiply_reduce_fusion.1
  295.2 0.0 copy-start.2
  295.2 51.2 %all-gather.5.cloned.1.call-done = bf16[4,1024,1024]{2,1,0:T(8,128)(2,1)} async-done(((bf16[4,32,1024]{2,1,0:T(8,128)(2,1)}), bf16[4,1024,1024]{2,1,0:T(8,128)(2,1)}) %all-gather.5.cloned.1.call-update) | async-done | bytes 8388624 | tf_op jit(solution)/shard_map/all_gather | solution.py:59
  346.4 0.0 copy-done
  346.4 8.9 %multiply_reduce_fusion = (f32[4]{0:T(128)S(1)}, f32[4,32,1024]{2,1,0:T(8,128)S(1)}) fusion(bf16[4,1024,1024]{2,1,0:T(8,128)(2,1)} %param.16, bf16[4,32,1024]{2,1,0:T(8,128)(2,1)S(1)} %copy-done, bf16[4,1024,1024]{2,1,0:T(8,128)(2,1)} %all-gather.5.cloned.1.call-done), kind=kOutput, calls=%fused_computation.21 | convolution fusion | flops 537264128 | bytes 17563664 | tf_op jit(solution)/shard_map/crk,ckm->crm/dot_general | solution.py:80
  355.2 0.0 copy-start.5
  355.2 31.0 %all-gather.1 = f32[32,2,4]{2,1,0:T(2,128)S(1)} all-gather(f32[1,2,4]{2,1,0:T(2,128)S(1)} %maximum_bitcast_fusion), channel_id=2, replica_groups=mesh['dp'=32,'mp'=8] {'dp'}, dimensions={0}, use_global_device_ids=true | all-gather | bytes 1056 | tf_op jit(solution)/shard_map/all_gather | solution.py:88
  386.3 0.1 multiply_convert_fusion
  386.5 0.9 copy.33
  387.4 15.5 %all-to-all-start.1 = ((bf16[4,32,8,128]{3,0,1,2:T(4,128)(2,1)}), bf16[4,32,8,128]{3,0,1,2:T(4,128)(2,1)S(1)}, u32[]{:S(2)}, u32[]{:S(2)}) async-start(bf16[4,32,8,128]{3,0,1,2:T(4,128)(2,1)} %copy.33), calls=%async_computation.2 | async-start | bytes 524288 | tf_op jit(solution)/shard_map/all_to_all | solution.py:95
  402.8 0.0 copy-done.2
  402.9 0.0 copy-start.1
  402.9 0.0 copy-start.8
  402.9 6.9 %fusion.1 = f32[4,32,1024]{2,1,0:T(8,128)} fusion(f32[4,32,1024]{2,1,0:T(8,128)S(1)} %copy-done.2, bf16[4,1024,1024]{2,1,0:T(8,128)(2,1)} %all-gather.5.cloned.1.call-done, pred[4]{0:T(512)(128)(4,1)S(1)} %broadcast_compare_fusion, bf16[4,32,8,128]{3,1,0,2:T(8,128)(2,1)S(1)} %all_to_all.10), kind=kOutput, calls=%fused_computation.3 | convolution fusion | flops 268828672 | bytes 9699332 | tf_op jit(solution)/shard_map/crk,cnk->crn/dot_general | solution.py:60
  409.8 0.0 copy-done.5
  409.8 0.0 copy-done.1
  409.8 2.6 fusion.3
  412.4 0.0 all-to-all-done.1
  412.4 0.0 copy-done.8
  412.4 0.3 fusion.5
  412.7 0.7 copy.36
  (6 shorter events, 0.2 us)
Async XLA Ops:
  7.2 339.2 %copy-start = (bf16[4,32,1024]{2,1,0:T(8,128)(2,1)S(1)}, bf16[4,32,1024]{2,1,0:T(8,128)(2,1)}, u32[]{:S(2)}) copy-start(bf16[4,32,1024]{2,1,0:T(8,128)(2,1)} %param.15) | copy-start | bytes 786436
  7.2 285.9 %copy-start.6 = (f32[9216]{0:T(1024)S(1)}, f32[9216]{0:T(1024)}, u32[]{:S(2)}) copy-start(f32[9216]{0:T(1024)} %param.21) | copy-start | bytes 110596
  7.2 285.9 %copy-start.7 = (f32[9216]{0:T(1024)S(1)}, f32[9216]{0:T(1024)}, u32[]{:S(2)}) copy-start(f32[9216]{0:T(1024)} %param.20) | copy-start | bytes 110596
  7.2 286.6 %copy-start.3 = (f32[4,32,1024]{2,1,0:T(8,128)S(1)}, f32[4,32,1024]{2,1,0:T(8,128)}, u32[]{:S(2)}) copy-start(f32[4,32,1024]{2,1,0:T(8,128)} %param.18) | copy-start | bytes 1572868
  7.2 286.6 %copy-start.4 = (f32[4,32,1024]{2,1,0:T(8,128)S(1)}, f32[4,32,1024]{2,1,0:T(8,128)}, u32[]{:S(2)}) copy-start(f32[4,32,1024]{2,1,0:T(8,128)} %param.17) | copy-start | bytes 1572868
  7.2 225.5 %reduce-scatter.2.cloned.1.call-start = ((), (), s32[]{:S(2)}) async-start(), calls=%async_computation.3 | async-start | bytes 4325376 | tf_op jit(solution)/shard_map/reduce_scatter | solution.py:44
  8.0 338.4 %all-gather.5.cloned.1.call-start = ((), (), s32[]{:S(2)}) async-start(), calls=%async_computation.4 | async-start | bytes 8650752 | tf_op jit(solution)/shard_map/all_gather | solution.py:59
  295.2 107.7 %copy-start.2 = (f32[4,32,1024]{2,1,0:T(8,128)S(1)}, f32[4,32,1024]{2,1,0:T(8,128)}, u32[]{:S(2)}) copy-start(f32[4,32,1024]{2,1,0:T(8,128)} %param.13) | copy-start | bytes 1572868
  355.2 54.6 %copy-start.5 = (f32[4,32,1024]{2,1,0:T(8,128)S(1)}, f32[4,32,1024]{2,1,0:T(8,128)}, u32[]{:S(2)}) copy-start(f32[4,32,1024]{2,1,0:T(8,128)} %param.14) | copy-start | bytes 1572868
  387.4 25.0 %all-to-all-start.1 = ((bf16[4,32,8,128]{3,0,1,2:T(4,128)(2,1)}), bf16[4,32,8,128]{3,0,1,2:T(4,128)(2,1)S(1)}, u32[]{:S(2)}, u32[]{:S(2)}) async-start(bf16[4,32,8,128]{3,0,1,2:T(4,128)(2,1)} %copy.33), calls=%async_computation.2 | async-start | bytes 524288 | tf_op jit(solution)/shard_map/all_to_all | solution.py:95
  402.9 6.9 %copy-start.1 = (bf16[4,1024,1024]{2,1,0:T(8,128)(2,1)S(1)}, bf16[4,1024,1024]{2,1,0:T(8,128)(2,1)}, u32[]{:S(2)}) copy-start(bf16[4,1024,1024]{2,1,0:T(8,128)(2,1)} %all-gather.5.cloned.1.call-done) | copy-start | bytes 25165828
  402.9 9.6 %copy-start.8 = (s32[16]{0:T(128)S(1)}, s32[16]{0:T(128)}, u32[]{:S(2)}) copy-start(s32[16]{0:T(128)} %param.12) | copy-start | bytes 196
Sparse Core Ops, SparseCore 0:
  12.0 220.7 reduce-scatter.1
  251.3 94.9 all-gather.4
where the time goes:
time: 421 us; the launch traced here: 420 us
  waiting for transfers between devices  276 us (66%)
  blocking collectives  87.3 us (21%)
  matrix products  19.8 us (5%)
  starting transfers between devices  15.5 us (4%)
  between operations  14.2 us (3%)
  other arithmetic  5.23 us (1%)
    reduce_scatter x1, waiting for transfers between devices, body(): lax.psum_scatter(grad_parts[0].astype(jnp.float32).astype(jnp.bfloat16),...  224 us
    all_gather x1, waiting for transfers between devices, body(): shard_rows = lax.all_gather(rounded_rows, 'dp', axis=1, tiled=True)  51.2 us
    all_gather x1, blocking collectives, body(): vec_all = lax.all_gather(vec_grad[0], 'dp')  39.8 us
    all_gather x1, blocking collectives, body(): squares = lax.all_gather(jnp.stack([square_adam, square_pre]), 'dp')  31 us
    all_to_all x1, blocking collectives, body(): lax.all_to_all(outgoing.astype(jnp.bfloat16), 'mp', split_axis=2, concat_...  16.5 us
    all_to_all x1, starting transfers between devices, body(): lax.all_to_all(update_rows.reshape(slot_count, row_count, owner_count, co...  15.5 us
    dot_general x1, matrix products, body(): jnp.einsum('crk,ckm->crm', applied_acc.astype(jnp.bfloat16), right_root,...  8.86 us
  transfers between devices with their start and end apart: 3, of which 2 were waited for; matrix products, arithmetic and copies ran while one was open for 3% of the time, Pallas kernels for 0%

commit v1 on v0

--- a/solution.py
+++ b/solution.py
@@ -56,7 +56,9 @@
     mine = lax.dynamic_index_in_dim(selector, my_owner, 0, keepdims=False)
     used_mask = (jnp.sum(mine, axis=1) > 0.5)[:, None, None]
     rounded_rows = grad_rows.astype(jnp.bfloat16)
-    shard_rows = lax.all_gather(rounded_rows, "dp", axis=1, tiled=True)
+    shard_rows = jnp.concatenate(
+        lax.all_to_all(jnp.stack([rounded_rows] * lax.axis_size("dp")), "dp", 0, 0), axis=1
+    )
     left_part = jnp.einsum(
         "crk,cnk->crn", rounded_rows, shard_rows, preferred_element_type=jnp.float32
     )

time: 421 us -> 585 us (1.39)
  blocking collectives: 87.3 us -> 267 us
  waiting for transfers between devices: 276 us -> 225 us
  starting transfers between devices: 15.5 us -> 39.9 us
  local copies, waits for them, and re-layouts: 2.48 us -> 14.5 us
    all_gather x1, blocking collectives: 39.8 us -> 220 us  [body(): vec_all = lax.all_gather(vec_grad[0], 'dp')]
    all_gather x1 -> x0, waiting for transfers between devices: 51.2 us -> none  [body(): shard_rows = lax.all_gather(rounded_rows, 'dp', axis=1, tiled=True)]
    all_to_all x1, starting transfers between devices: 15.5 us -> 33.2 us  [body(): lax.all_to_all(update_rows.reshape(slot_count, row_count, owner_count, co...]
    reshape x0 -> x1, local copies, waits for them, and re-layouts: none -> 8.46 us  [body(): jnp.concatenate(lax.all_to_all(jnp.stack([rounded_rows] * lax.axis_size('...]
    all_to_all x0 -> x1, starting transfers between devices: none -> 6.62 us  [body(): lax.all_to_all(jnp.stack([rounded_rows] * lax.axis_size('dp')), 'dp', 0, 0)]
  transfers between devices with their start and end apart: 3 -> 3, of which waited for: 2 -> 1; matrix products, arithmetic and copies ran while one was open for 3% -> 2% of each run, Pallas kernels for 0% -> 0%
where the time goes in v1:
time: 585 us
  blocking collectives  267 us (46%)
  waiting for transfers between devices  225 us (38%)
  starting transfers between devices  39.9 us (7%)
  matrix products  19.9 us (3%)
  local copies, waits for them, and re-layouts  14.5 us (2%)
  between operations  14.2 us (2%)
    reduce_scatter x1, waiting for transfers between devices, body(): lax.psum_scatter(grad_parts[0].astype(jnp.float32).astype(jnp.bfloat16),...  224 us
    all_gather x1, blocking collectives, body(): vec_all = lax.all_gather(vec_grad[0], 'dp')  220 us
    all_to_all x1, starting transfers between devices, body(): lax.all_to_all(update_rows.reshape(slot_count, row_count, owner_count, co...  33.2 us
    all_gather x1, blocking collectives, body(): squares = lax.all_gather(jnp.stack([square_adam, square_pre]), 'dp')  30.7 us
    all_to_all x1, blocking collectives, body(): lax.all_to_all(outgoing.astype(jnp.bfloat16), 'mp', split_axis=2, concat_...  16.5 us
  transfers between devices with their start and end apart: 3, of which 1 were waited for; matrix products, arithmetic and copies ran while one was open for 2% of the time, Pallas kernels for 0%

profile of v1, /device:TPU:1, one launch (start us, length us, event | category | flops | bytes accessed | tf_op | source)
XLA Modules:
  0.0 584.9 jit_solution(10811623409406870568)
XLA Ops:
  7.2 0.0 copy-start
  7.2 0.0 reduce-scatter.2.cloned.1.call-start
  7.2 0.7 reduce-scatter.2.cloned.1.call-update
  7.9 0.9 convert_reduce_fusion.1
  8.8 223.9 %reduce-scatter.2.cloned.1.call-done = bf16[16,32,128]{2,1,0:T(8,128)(2,1)} async-done(((bf16[16,1024,128]{2,1,0:T(8,128)(2,1)}), bf16[16,32,128]{2,1,0:T(8,128)(2,1)}) %reduce-scatter.2.cloned.1.call-update) | async-done | bytes 131088 | tf_op jit(solution)/shard_map/reduce_scatter | solution.py:44
  232.7 1.1 fusion.4
  233.9 16.5 %all_to_all.15 = bf16[4,32,8,128]{3,1,0,2:T(8,128)(2,1)S(1)} all-to-all(bf16[4,32,8,128]{3,1,0,2:T(8,128)(2,1)S(1)} %copy.32), channel_id=1, replica_groups=mesh['dp'=32,'mp'=8] {'mp'}, dimensions={2} | all-to-all | bytes 524288 | tf_op jit(solution)/shard_map/all_to_all | solution.py:52
  250.4 4.3 stack.8
  254.7 0.0 copy-start.9
  254.7 0.0 copy-start.6
  254.7 0.0 copy-start.7
  254.7 0.0 copy-start.8
  254.7 0.0 copy-start.3
  254.7 0.0 copy-start.4
  254.8 6.6 %all-to-all-start.1 = ((bf16[32,4,32,1024]{3,2,1,0:T(8,128)(2,1)}), bf16[32,4,32,1024]{3,2,1,0:T(8,128)(2,1)}, u32[]{:S(2)}, u32[]{:S(2)}) async-start(bf16[32,4,32,1024]{3,2,1,0:T(8,128)(2,1)} %stack.8), calls=%async_computation.2 | async-start | bytes 16777216 | tf_op jit(solution)/shard_map/all_to_all | solution.py:60
  261.4 0.0 copy-done.9
  261.4 0.1 dynamic-slice_reduce_fusion
  261.5 0.0 copy-done.6
  261.5 220.2 %all-gather.2 = bf16[32,1,9216]{2,1,0:T(2,128)(2,1)S(1)} all-gather(bf16[1,1,9216]{2,1,0:T(2,128)(2,1)S(1)} %bitcast.60), channel_id=1, replica_groups=mesh['dp'=32,'mp'=8] {'dp'}, dimensions={0}, use_global_device_ids=true | all-gather | bytes 608256 | tf_op jit(solution)/shard_map/all_gather | solution.py:92
  481.7 1.3 convert_reduce_fusion
  483.1 0.0 copy-done.7
  483.1 0.0 copy-done.8
  483.1 0.6 divide_convert_fusion
  483.7 0.0 copy-done.3
  483.7 0.0 copy-done.4
  483.7 1.4 multiply_reduce_fusion.1
  485.1 0.0 all-to-all-done.1
  485.1 8.5 %copy.34 = bf16[4,32,32,1024]{3,2,1,0:T(8,128)(2,1)} copy(bf16[4,32,32,1024]{3,2,0,1:T(8,128)(2,1)} %bitcast.6) | data formatting | bytes 16777216 | tf_op jit(solution)/shard_map/reshape | solution.py:59
  493.6 0.0 copy-done
  493.6 0.0 copy-start.2
  493.6 8.9 %multiply_reduce_fusion = (f32[4]{0:T(128)S(1)}, f32[4,32,1024]{2,1,0:T(8,128)S(1)}) fusion(bf16[4,1024,1024]{2,1,0:T(8,128)(2,1)} %param.16, bf16[4,32,1024]{2,1,0:T(8,128)(2,1)S(1)} %copy-done, bf16[4,1024,1024]{2,1,0:T(8,128)(2,1)} %bitcast.54), kind=kOutput, calls=%fused_computation.21 | convolution fusion | flops 537264128 | bytes 17563664 | tf_op jit(solution)/shard_map/crk,ckm->crm/dot_general | solution.py:82
  502.5 0.0 copy-start.5
  502.5 30.7 %all-gather.1 = f32[32,2,4]{2,1,0:T(2,128)S(1)} all-gather(f32[1,2,4]{2,1,0:T(2,128)S(1)} %maximum_bitcast_fusion), channel_id=2, replica_groups=mesh['dp'=32,'mp'=8] {'dp'}, dimensions={0}, use_global_device_ids=true | all-gather | bytes 1056 | tf_op jit(solution)/shard_map/all_gather | solution.py:90
  533.2 0.1 multiply_convert_fusion
  533.4 0.9 copy.35
  534.3 33.2 %all-to-all-start.2 = ((bf16[4,32,8,128]{3,0,1,2:T(4,128)(2,1)}), bf16[4,32,8,128]{3,0,1,2:T(4,128)(2,1)S(1)}, u32[]{:S(2)}, u32[]{:S(2)}) async-start(bf16[4,32,8,128]{3,0,1,2:T(4,128)(2,1)} %copy.35), calls=%async_computation.3 | async-start | bytes 524288 | tf_op jit(solution)/shard_map/all_to_all | solution.py:97
  567.5 0.0 copy-done.2
  567.5 0.0 copy-start.1
  567.5 6.9 %fusion.1 = f32[4,32,1024]{2,1,0:T(8,128)} fusion(f32[4,32,1024]{2,1,0:T(8,128)S(1)} %copy-done.2, bf16[4,1024,1024]{2,1,0:T(8,128)(2,1)} %bitcast.55, pred[4]{0:T(512)(128)(4,1)S(1)} %broadcast_compare_fusion, bf16[4,32,8,128]{3,1,0,2:T(8,128)(2,1)S(1)} %all_to_all.15), kind=kOutput, calls=%fused_computation.3 | convolution fusion | flops 268828672 | bytes 9699332 | tf_op jit(solution)/shard_map/crk,cnk->crn/dot_general | solution.py:62
  574.4 0.0 copy-done.5
  574.4 0.0 copy-done.1
  574.4 2.6 fusion.3
  577.0 0.0 all-to-all-done.2
  577.0 0.3 fusion.5
  577.3 0.7 copy.38
  (8 shorter events, 0.2 us)
Async XLA Ops:
  7.2 486.4 %copy-start = (bf16[4,32,1024]{2,1,0:T(8,128)(2,1)S(1)}, bf16[4,32,1024]{2,1,0:T(8,128)(2,1)}, u32[]{:S(2)}) copy-start(bf16[4,32,1024]{2,1,0:T(8,128)(2,1)} %param.15) | copy-start | bytes 786436
  7.2 225.5 %reduce-scatter.2.cloned.1.call-start = ((), (), s32[]{:S(2)}) async-start(), calls=%async_computation.4 | async-start | bytes 4325376 | tf_op jit(solution)/shard_map/reduce_scatter | solution.py:44
  254.7 6.7 %copy-start.9 = (s32[16]{0:T(128)S(1)}, s32[16]{0:T(128)}, u32[]{:S(2)}) copy-start(s32[16]{0:T(128)} %param.12) | copy-start | bytes 196
  254.7 6.8 %copy-start.6 = (bf16[1,9216]{1,0:T(2,128)(2,1)S(1)}, bf16[1,9216]{1,0:T(2,128)(2,1)}, u32[]{:S(2)}) copy-start(bf16[1,9216]{1,0:T(2,128)(2,1)} %param.19) | copy-start | bytes 55300
  254.7 228.3 %copy-start.7 = (f32[9216]{0:T(1024)S(1)}, f32[9216]{0:T(1024)}, u32[]{:S(2)}) copy-start(f32[9216]{0:T(1024)} %param.21) | copy-start | bytes 110596
  254.7 228.3 %copy-start.8 = (f32[9216]{0:T(1024)S(1)}, f32[9216]{0:T(1024)}, u32[]{:S(2)}) copy-start(f32[9216]{0:T(1024)} %param.20) | copy-start | bytes 110596
  254.7 229.0 %copy-start.3 = (f32[4,32,1024]{2,1,0:T(8,128)S(1)}, f32[4,32,1024]{2,1,0:T(8,128)}, u32[]{:S(2)}) copy-start(f32[4,32,1024]{2,1,0:T(8,128)} %param.18) | copy-start | bytes 1572868
  254.7 229.0 %copy-start.4 = (f32[4,32,1024]{2,1,0:T(8,128)S(1)}, f32[4,32,1024]{2,1,0:T(8,128)}, u32[]{:S(2)}) copy-start(f32[4,32,1024]{2,1,0:T(8,128)} %param.17) | copy-start | bytes 1572868
  254.8 230.3 %all-to-all-start.1 = ((bf16[32,4,32,1024]{3,2,1,0:T(8,128)(2,1)}), bf16[32,4,32,1024]{3,2,1,0:T(8,128)(2,1)}, u32[]{:S(2)}, u32[]{:S(2)}) async-start(bf16[32,4,32,1024]{3,2,1,0:T(8,128)(2,1)} %stack.8), calls=%async_computation.2 | async-start | bytes 16777216 | tf_op jit(solution)/shard_map/all_to_all | solution.py:60
  493.6 73.9 %copy-start.2 = (f32[4,32,1024]{2,1,0:T(8,128)S(1)}, f32[4,32,1024]{2,1,0:T(8,128)}, u32[]{:S(2)}) copy-start(f32[4,32,1024]{2,1,0:T(8,128)} %param.13) | copy-start | bytes 1572868
  502.5 71.9 %copy-start.5 = (f32[4,32,1024]{2,1,0:T(8,128)S(1)}, f32[4,32,1024]{2,1,0:T(8,128)}, u32[]{:S(2)}) copy-start(f32[4,32,1024]{2,1,0:T(8,128)} %param.14) | copy-start | bytes 1572868
  534.3 42.8 %all-to-all-start.2 = ((bf16[4,32,8,128]{3,0,1,2:T(4,128)(2,1)}), bf16[4,32,8,128]{3,0,1,2:T(4,128)(2,1)S(1)}, u32[]{:S(2)}, u32[]{:S(2)}) async-start(bf16[4,32,8,128]{3,0,1,2:T(4,128)(2,1)} %copy.35), calls=%async_computation.3 | async-start | bytes 524288 | tf_op jit(solution)/shard_map/all_to_all | solution.py:97
  567.5 6.9 %copy-start.1 = (bf16[4,32,32,1024]{3,2,1,0:T(8,128)(2,1)S(1)}, bf16[4,32,32,1024]{3,2,1,0:T(8,128)(2,1)}, u32[]{:S(2)}) copy-start(bf16[4,32,32,1024]{3,2,1,0:T(8,128)(2,1)} %copy.34) | copy-start | bytes 25165828
Sparse Core Ops, SparseCore 0:
  11.9 220.7 reduce-scatter.1
